TPU v7x, 512 devices: a whole 4x4x16 slice. The times are simulated.
512 devices in a mesh: rows: 32 (over z_lo, y), blk: 16 (over x, z_hi, core).
Axes of the slice: x: 4, y: 4, z: 16 (z_hi: 2, z_lo: 8; z = z_hi * 8 + z_lo), core: 2. Of those that a mesh axis runs over, the one named last changes fastest.
Arguments:
- features: bfloat16 [131072, 1024], P(('rows', 'blk')), may hold values from -6 to 6
- tiles: bfloat16 [512, 7, 256, 256], P(('rows', 'blk')), may hold values from -0.1875 to 0.1875
- tile_cols: int32 [512, 7], P(('rows', 'blk')), may hold values from 0 to 511, as said below
- tile_count: int32 [512], P(('rows', 'blk')), may hold values from 1 to 7
- weight: bfloat16 [1024, 1024], P(('rows', 'blk')), may hold values from -0.1875 to 0.1875
- cotangent: bfloat16 [131072, 1024], P(('rows', 'blk')), may hold values from -0.0625 to 0.0625
Outputs:
- output: bfloat16 [131072, 1024], P(('rows', 'blk'))
- weight_grad: float32 [1024, 1024], P(('rows', 'blk'))
Inputs may be any that keep to these rules, and one draw needn't show every extreme that they name: For each row block g, the first tile_count[g] entries of tile_cols[g] are distinct blocks of g's group of 16 blocks (blocks 16 * (g // 16) onward), each at most 3 positions from g around that group, g itself among them; the later entries are also blocks of that group and carry no tile.
All inputs are finite; a program needn't handle non-finite values.
Results may differ from a plain program's by a relative error of at most 0.0054.
Values may be sent and summed in bfloat16 or wider, within the bound.
A program may use at most 64 MiB of HBM per device.

v0:
```python
import jax
import jax.numpy as jnp
from jax import lax
from jax.sharding import PartitionSpec as P


def passed_along(value, axis, by):
    length = lax.axis_size(axis)
    return lax.ppermute(value, axis, [(i, (i + by) % length) for i in range(length)])


def local(features, tiles, tile_cols, tile_count, weight, cotangent):
    cycle_len = lax.axis_size("blk")
    position = lax.axis_index("blk")
    per_dev = tiles.shape[0]
    slot_total = tiles.shape[1]
    tile_side = tiles.shape[2]
    group_len = cycle_len * per_dev
    slot_ids = jnp.arange(slot_total, dtype=jnp.int32)
    columns = tile_cols % group_len

    def apply_panel(totals, panel_now, source):
        running = totals[0]
        in_use = slot_ids < tile_count[0]
        wanted = source * per_dev + 0
        match = jnp.logical_and(in_use, columns[0] == wanted)
        present = jnp.any(match)
        chosen_slot = jnp.sum(jnp.where(match, slot_ids, 0))
        chosen = lax.dynamic_index_in_dim(tiles[0], chosen_slot, 0, keepdims=False)
        rows_there = panel_now

        def multiply(chosen=chosen, rows_there=rows_there):
            return jnp.dot(chosen, rows_there, preferred_element_type=jnp.float32)

        def nothing():
            return jnp.zeros(running.shape, jnp.float32)

        running = running + lax.cond(present, multiply, nothing)
        updated = [running]
        return tuple(updated)

    empty = jnp.zeros((tile_side, features.shape[1]), jnp.float32)
    totals = tuple((empty for block_here in range(per_dev)))
    totals = apply_panel(totals, features, position)
    reach_blocks = min(3, (group_len - 1) // 2)
    reach_dev = (reach_blocks + per_dev - 1) // per_dev
    from_left = features
    from_right = features
    for offset in range(1, reach_dev + 1):
        from_left = passed_along(from_left, "blk", 1)
        totals = apply_panel(totals, from_left, (position - offset + cycle_len) % cycle_len)
        from_right = passed_along(from_right, "blk", -1)
        totals = apply_panel(totals, from_right, (position + offset) % cycle_len)
    aggregated = totals[0].astype(jnp.bfloat16)
    pre_act = lax.dot_general(
        aggregated,
        lax.all_gather(weight, ("rows", "blk"), axis=0, tiled=True),
        (((1,), (1,)), ((), ())),
        preferred_element_type=jnp.float32,
    )
    output = jax.nn.silu(pre_act).astype(jnp.bfloat16)
    sigmoid_y = jax.nn.sigmoid(pre_act)
    grad_pre = (
        cotangent.astype(jnp.float32) * sigmoid_y * (1.0 + pre_act * (1.0 - sigmoid_y))
    ).astype(jnp.bfloat16)
    weight_grad = lax.psum_scatter(
        lax.dot_general(
            grad_pre, aggregated, (((0,), (0,)), ((), ())), preferred_element_type=jnp.float32
        ),
        ("rows", "blk"),
        scatter_dimension=0,
        tiled=True,
    )
    return (output, weight_grad)


def solution(mesh):
    in_specs = (
        P(("rows", "blk"), None),
        P(("rows", "blk"), None, None, None),
        P(("rows", "blk"), None),
        P(("rows", "blk")),
        P(("rows", "blk"), None),
        P(("rows", "blk"), None),
    )
    out_specs = (P(("rows", "blk"), None), P(("rows", "blk"), None))
    return jax.shard_map(local, mesh=mesh, in_specs=in_specs, out_specs=out_specs, check_vma=False)
```

profile of v0, /device:TPU:2, one launch (start us, length us, event | category | flops | bytes accessed | tf_op | source)
XLA Modules:
  0.0 1387.6 jit_solution(14543954781679902342)
XLA Ops:
  7.2 0.0 all-gather.3.cloned.1.call-start
  7.2 0.7 all-gather.3.cloned.1.call-update
  7.9 0.0 all-reduce.3.cloned.1.call-start
  7.9 1.9 collective-permute-start
  9.9 15.1 %collective-permute-start.1 = (bf16[256,1024]{1,0:T(8,128)(2,1)}, bf16[256,1024]{1,0:T(8,128)(2,1)S(1)}, u32[]{:S(2)}, u32[]{:S(2)}) collective-permute-start(bf16[256,1024]{1,0:T(8,128)(2,1)} %param.20), channel_id=1, source_target_pairs={{0,15},{1,0},{2,1},{3,2},{4,3},{5,4},{6,5},{7,6},{8,7},{9,8},{10,9... | collective-permute-start | bytes 1572872 | tf_op jit(solution)/shard_map/ppermute | solution.py:9
  25.0 5.4 collective-permute-done
  30.4 0.0 copy-start
  30.4 0.8 copy-done
  31.2 21.4 %collective-permute-start.2 = (bf16[256,1024]{1,0:T(8,128)(2,1)S(1)}, bf16[256,1024]{1,0:T(8,128)(2,1)}, u32[]{:S(2)}, u32[]{:S(2)}) collective-permute-start(bf16[256,1024]{1,0:T(8,128)(2,1)S(1)} %collective-permute-done), channel_id=1, source_target_pairs={{0,1},{1,2},{2,3},{3,4},{4,5},{5,6},{6,7},{7,8},{8,9},{9,10},{10,1... | collective-permute-start | bytes 1572872 | tf_op jit(solution)/shard_map/ppermute | solution.py:9
  52.6 6.6 collective-permute-done.1
  59.2 13.5 collective-permute-start.3
  72.7 6.4 collective-permute-done.2
  79.2 8.0 collective-permute-start.4
  87.2 0.5 collective-permute-done.3
  87.7 13.8 collective-permute-start.5
  102.2 1.4 fusion.32
  103.5 0.8 fusion.33
  108.6 3.8 conditional.7
  108.6 0.6 select_reduce_fusion
  111.0 1.4 fusion
  112.4 0.1 conditional.9
  112.4 0.1 broadcast.44
  112.5 0.1 conditional.8
  112.6 0.1 broadcast.43
  112.7 1.1 conditional.10
  112.7 1.1 broadcast.45
  113.8 1.1 conditional.11
  113.8 1.1 broadcast.46
  114.9 2.3 collective-permute-done.4
  117.2 1.1 conditional.12
  117.2 1.1 broadcast.47
  118.3 13.6 collective-permute-done.5
  132.0 1.1 conditional.13
  132.0 1.1 broadcast.48
  133.1 3.6 add_convert_fusion
  136.7 0.0 copy-start.1
  136.7 747.7 %all-gather.3.cloned.1.call-done = bf16[512,2,1024]{2,1,0:T(2,128)(2,1)} async-done(((bf16[1,2,1024]{2,1,0:T(2,128)(2,1)}), bf16[512,2,1024]{2,1,0:T(2,128)(2,1)}) %all-gather.3.cloned.1.call-update) | async-done | bytes 2097168 | tf_op jit(solution)/shard_map/all_gather | solution.py:57
  884.4 2.7 reshape.33
  887.2 0.0 copy-done.1
  887.2 0.0 copy-start.2
  887.2 1.6 multiply_convert_fusion.1
  888.8 0.0 copy-done.2
  888.8 3.0 fusion.28
  891.9 0.0 all-reduce.3.cloned.1.call-update
  891.9 487.5 %all-reduce.3.cloned.1.call-done = f32[1024,1024]{1,0:T(8,128)} async-done(((f32[1024,1024]{1,0:T(8,128)}), f32[1024,1024]{1,0:T(8,128)}) %all-reduce.3.cloned.1.call-update) | async-done | bytes 4194320
  1379.4 1.4 constant_dynamic-slice_fusion
  (7 shorter events, 0.0 us)
Async XLA Ops:
  7.2 877.3 %all-gather.3.cloned.1.call-start = ((), (), s32[]{:S(2)}) async-start(), calls=%async_computation | async-start | bytes 2101248 | tf_op jit(solution)/shard_map/all_gather | solution.py:57
  7.9 1371.5 %all-reduce.3.cloned.1.call-start = ((), (), s32[]{:S(2)}) async-start(), calls=%async_computation.1 | async-start | bytes 8388608
  7.9 22.5 %collective-permute-start = (bf16[256,1024]{1,0:T(8,128)(2,1)}, bf16[256,1024]{1,0:T(8,128)(2,1)S(1)}, u32[]{:S(2)}, u32[]{:S(2)}) collective-permute-start(bf16[256,1024]{1,0:T(8,128)(2,1)} %param.20), channel_id=1, source_target_pairs={{0,1},{1,2},{2,3},{3,4},{4,5},{5,6},{6,7},{7,8},{8,9},{9,10},{10,1... | collective-permute-start | bytes 1572872 | tf_op jit(solution)/shard_map/ppermute | solution.py:9
  9.9 49.4 %collective-permute-start.1 = (bf16[256,1024]{1,0:T(8,128)(2,1)}, bf16[256,1024]{1,0:T(8,128)(2,1)S(1)}, u32[]{:S(2)}, u32[]{:S(2)}) collective-permute-start(bf16[256,1024]{1,0:T(8,128)(2,1)} %param.20), channel_id=1, source_target_pairs={{0,15},{1,0},{2,1},{3,2},{4,3},{5,4},{6,5},{7,6},{8,7},{9,8},{10,9... | collective-permute-start | bytes 1572872 | tf_op jit(solution)/shard_map/ppermute | solution.py:9
  30.4 0.8 copy-start
  31.2 47.9 %collective-permute-start.2 = (bf16[256,1024]{1,0:T(8,128)(2,1)S(1)}, bf16[256,1024]{1,0:T(8,128)(2,1)}, u32[]{:S(2)}, u32[]{:S(2)}) collective-permute-start(bf16[256,1024]{1,0:T(8,128)(2,1)S(1)} %collective-permute-done), channel_id=1, source_target_pairs={{0,1},{1,2},{2,3},{3,4},{4,5},{5,6},{6,7},{7,8},{8,9},{9,10},{10,1... | collective-permute-start | bytes 1572872 | tf_op jit(solution)/shard_map/ppermute | solution.py:9
  59.2 28.4 %collective-permute-start.3 = (bf16[256,1024]{1,0:T(8,128)(2,1)S(1)}, bf16[256,1024]{1,0:T(8,128)(2,1)}, u32[]{:S(2)}, u32[]{:S(2)}) collective-permute-start(bf16[256,1024]{1,0:T(8,128)(2,1)S(1)} %collective-permute-done.1), channel_id=1, source_target_pairs={{0,15},{1,0},{2,1},{3,2},{4,3},{5,4},{6,5},{7,6},{8,7},{9,8},{10,9... | collective-permute-start | bytes 1572872 | tf_op jit(solution)/shard_map/ppermute | solution.py:9
  79.2 38.0 %collective-permute-start.4 = (bf16[256,1024]{1,0:T(8,128)(2,1)}, bf16[256,1024]{1,0:T(8,128)(2,1)}, u32[]{:S(2)}, u32[]{:S(2)}) collective-permute-start(bf16[256,1024]{1,0:T(8,128)(2,1)} %collective-permute-done.2), channel_id=1, source_target_pairs={{0,1},{1,2},{2,3},{3,4},{4,5},{5,6},{6,7},{7,8},{8,9},{9,10},{10,1... | collective-permute-start | bytes 1572872 | tf_op jit(solution)/shard_map/ppermute | solution.py:9
  87.7 44.3 %collective-permute-start.5 = (bf16[256,1024]{1,0:T(8,128)(2,1)}, bf16[256,1024]{1,0:T(8,128)(2,1)}, u32[]{:S(2)}, u32[]{:S(2)}) collective-permute-start(bf16[256,1024]{1,0:T(8,128)(2,1)} %collective-permute-done.3), channel_id=1, source_target_pairs={{0,15},{1,0},{2,1},{3,2},{4,3},{5,4},{6,5},{7,6},{8,7},{9,8},{10,9... | collective-permute-start | bytes 1572872 | tf_op jit(solution)/shard_map/ppermute | solution.py:9
  136.7 750.5 %copy-start.1 = (bf16[256,1024]{1,0:T(8,128)(2,1)S(1)}, bf16[256,1024]{1,0:T(8,128)(2,1)}, u32[]{:S(2)}) copy-start(bf16[256,1024]{1,0:T(8,128)(2,1)} %add_convert_fusion) | copy-start | bytes 1572868
  887.2 1.6 copy-start.2
Sparse Core Ops, SparseCore 0:
  10.1 874.2 all-gather.2
  892.0 487.3 all-reduce.2
where the time goes:
time: 1390 us
  waiting for transfers between devices  1270 us (91%)
  starting transfers between devices  73.8 us (5%)
  between operations  19.2 us (1%)
    all_gather x1, waiting for transfers between devices, local(): lax.all_gather(weight, ('rows', 'blk'), axis=0, tiled=True)  748 us
    unnamed x3, waiting for transfers between devices  488 us
    ppermute x6, starting transfers between devices, passed_along(): lax.ppermute(value, axis, [(i, (i + by) % length) for i in range(length)])  73.7 us
    ppermute x6, waiting for transfers between devices, passed_along(): lax.ppermute(value, axis, [(i, (i + by) % length) for i in range(length)])  34.9 us
  transfers between devices with their start and end apart: 8, of which 8 were waited for; matrix products, arithmetic and copies ran while one was open for 1% of the time, Pallas kernels for 0%

commit v1 on v0

v1 whole, which is shorter than its diff:
```python
import functools

import jax
import jax.numpy as jnp
from jax import lax
from jax.experimental import pallas as pl
from jax.experimental.pallas import tpu as pltpu
from jax.sharding import PartitionSpec as P

MESH = pl.DeviceIdType.MESH
BF = jnp.bfloat16
F32 = jnp.float32
X, Y, Z, C = 4, 4, 16, 2
TILE = 256
F = 1024
SLOTS = 7
CHUNKS = 8
CROWS = TILE // CHUNKS
H = F // 2
PIECE = 2 * Z


def kernel(
    feat, tiles, cols, count, weight, cot, out, wgrad,
    fbuf, tbuf, tsel, cbuf, cperm, onehot, wz, wall, acc, agg, grad, gpart, outp, outv, dw,
    s1x, r1x, s1y, r1y, t2x, t2y, s2x, r2x, s2y, r2y, zs, zr,
    loc, f1s, f1r, f2s, f2r, f3s, f3r, f4s, f4r, f5s, f5r, f6s, f6r,
    wzs, wzr, wys, wyr, wxs, wxr, wps, wpr, ags, agr, gs, gr,
    a1s, a1r, b1s, b1r, a2s, a2r, b2s, b2r, z3s, z3r,
):
    row = lax.axis_index("rows")
    blk = lax.axis_index("blk")
    y = row % Y
    k = blk % C
    zh = (blk // C) % 2
    x = blk // (2 * C)
    z = zh * (Z // 2) + row // Y
    other = 1 - k

    def device(xx, yy, zz, cc):
        return ((zz % (Z // 2)) * Y + yy, (xx * 2 + zz // (Z // 2)) * C + cc)

    partner = device(x, y, z, other)
    far = device(x, y, (z + Z // 2) % Z, k)
    sign = 2 * k - 1
    side = device((x + sign + X) % X, y, z, other)
    step = 1 - 2 * zh
    onward = device((x + step + X) % X, y, z, k)

    def xpeer(d):
        return (x + d) % X

    def ypeer(d):
        return (y + d) % Y

    def zpeer(d):
        return (z + d) % Z

    def remote(src, dst, ss, rs, to):
        return pltpu.make_async_remote_copy(
            src_ref=src, dst_ref=dst, send_sem=ss, recv_sem=rs, device_id=to, device_id_type=MESH
        )

    barrier = pltpu.get_barrier_semaphore()

    def greet(to):
        pl.semaphore_signal(barrier, inc=1, device_id=to, device_id_type=MESH)

    greet(partner)
    greet(side)
    for d in range(1, X):
        greet(device(xpeer(d), y, z, k))
    for d in range(1, Y):
        greet(device(x, ypeer(d), z, k))

    @pl.loop(1, Z)
    def _(d):
        greet(device(x, y, zpeer(d), k))

    own = 4 + k
    load_w = pltpu.make_async_copy(weight, wz.at[z], loc.at[0])
    load_w.start()
    load_f = pltpu.make_async_copy(feat, fbuf.at[own], loc.at[1])
    load_f.start()
    load_t = pltpu.make_async_copy(tiles.at[0], tbuf, loc.at[2])
    load_t.start()
    load_c = pltpu.make_async_copy(cot, cbuf, loc.at[3])
    load_c.start()

    pl.semaphore_wait(barrier, 2 + (X - 1) + (Y - 1) + (Z - 1))

    def wz_copy(d, to):
        return remote(weight, wz.at[to], wzs.at[d], wzr.at[d], device(x, y, zpeer(d), k))

    @pl.loop(1, Z)
    def _(d):
        remote(weight, wz.at[z], wzs.at[d], wzr.at[d], device(x, y, zpeer(d), k)).start()

    same = jnp.where(zh == 1, 0, 2) + k
    cross = jnp.where(zh == 1, 2, 0) + k
    same_there = jnp.where(zh == 1, 2, 0) + k

    def f2(j):
        rows = pl.ds(j * CROWS, CROWS)
        return remote(feat.at[rows], fbuf.at[same_there, rows], f2s.at[j], f2r.at[j], far)

    @pl.loop(0, CHUNKS)
    def _(j):
        f2(j).start()

    f1 = remote(feat, fbuf.at[own], f1s, f1r, partner)
    f1.start()
    f3 = remote(feat, fbuf.at[6], f3s, f3r, side)
    f3.start()

    lane = lax.broadcasted_iota(jnp.int32, (1, F), 1)
    place = (
        (((lane >> 1) & 1) << 9)
        | (((lane >> 5) & 3) << 7)
        | (((lane >> 3) & 3) << 5)
        | (((lane >> 2) & 1) << 4)
        | (((lane >> 7) & 7) << 1)
        | (lane & 1)
    )

    @pl.loop(0, F // 64)
    def _(i):
        rows = lax.broadcasted_iota(jnp.int32, (64, F), 0) + i * 64
        onehot[pl.ds(pl.multiple_of(i * 64, 64), 64), :] = jnp.where(rows == place, 1.0, 0.0).astype(BF)

    load_t.wait()
    live = count[0]
    chip2 = blk - k
    slot_of = []
    for t in range(SLOTS):
        away = (cols[0, t] % (2 * X * C) - chip2 + 2 + 2 * X * C) % (2 * X * C)
        place_t = jnp.where(
            away < 2, away, jnp.where(away < 4, away + 2, jnp.where(away < 6, away - 2, 6))
        )
        slot_of.append(jnp.where(t < live, place_t, -1))
    for s in range(SLOTS):
        which = jnp.int32(0)
        found = jnp.int32(0)
        for t in range(SLOTS):
            hit = slot_of[t] == s
            which = jnp.where(hit, t, which)
            found = jnp.where(hit, 1, found)
        keep = jnp.full((TILE, TILE), found, jnp.int32) == 1
        tsel[:, s * TILE:(s + 1) * TILE] = jnp.where(keep, tbuf[which], jnp.zeros((TILE, TILE), BF))

    load_w.wait()

    @pl.loop(1, Z)
    def _(d):
        remote(weight, wz.at[zpeer(Z - d)], wzs.at[d], wzr.at[d], device(x, y, zpeer(Z - d), k)).wait_recv()

    wall[k, y, x] = wz[...].astype(F32).reshape(PIECE, F).astype(BF)

    def wy(d, dst):
        return remote(
            wall.at[k, dst, x], wall.at[k, dst, x], wys.at[d], wyr.at[d], device(x, ypeer(d), z, k)
        )

    for d in range(1, Y):
        wy(d, y).start()

    load_c.wait()
    for h in range(C):
        cperm[h] = lax.dot_general(
            cbuf[...], onehot[h * H:(h + 1) * H, :], (((1,), (1,)), ((), ())), preferred_element_type=F32
        ).astype(BF)

    for d in range(1, Y):
        wy(d, ypeer(Y - d)).wait_recv()

    def wx(d, dst):
        return remote(
            wall.at[k, :, dst], wall.at[k, :, dst], wxs.at[d], wxr.at[d], device(xpeer(d), y, z, k)
        )

    for d in range(1, X):
        wx(d, x).start()

    load_f.wait()
    remote(feat, fbuf.at[4 + other], f1s, f1r, partner).wait_recv()
    f3.wait_recv()

    @pl.loop(0, F // 256)
    def _(n):
        span = pl.ds(pl.multiple_of(n * 256, 256), 256)
        acc[:, span] = jnp.dot(
            tsel[:, 4 * TILE:], fbuf[4:, :, span].reshape(3 * TILE, 256), preferred_element_type=F32
        )

    def f4(j, slot):
        rows = pl.ds(j * CROWS, CROWS)
        return remote(fbuf.at[slot, rows], fbuf.at[slot, rows], f4s.at[j], f4r.at[j], partner)

    def f5(j, src, dst):
        rows = pl.ds(j * CROWS, CROWS)
        return remote(fbuf.at[src, rows], fbuf.at[dst, rows], f5s.at[j], f5r.at[j], onward)

    def f6(j, slot):
        rows = pl.ds(j * CROWS, CROWS)
        return remote(fbuf.at[slot, rows], fbuf.at[slot, rows], f6s.at[j], f6r.at[j], partner)

    def far_arrival(j):
        rows = pl.ds(j * CROWS, CROWS)
        remote(feat.at[rows], fbuf.at[same, rows], f2s.at[j], f2r.at[j], far).wait_recv()
        f4(j, same).start()
        f5(j, same, cross).start()

    def cross_arrival(j):
        f5(j, same, cross).wait_recv()
        f6(j, cross).start()

    far_arrival(0)

    @pl.loop(1, CHUNKS // 2)
    def _(j):
        far_arrival(j)
        cross_arrival(j - 1)

    for d in range(1, X):
        wx(d, xpeer(X - d)).wait_recv()
    wp = remote(wall.at[k], wall.at[k], wps, wpr, partner)
    wp.start()

    @pl.loop(CHUNKS // 2, CHUNKS)
    def _(j):
        far_arrival(j)
        cross_arrival(j - 1)

    cross_arrival(CHUNKS - 1)
    remote(wall.at[other], wall.at[other], wps, wpr, partner).wait_recv()

    @pl.loop(0, CHUNKS)
    def _(j):
        f4(j, same + other - k).wait_recv()
        f6(j, cross + other - k).wait_recv()

    @pl.loop(0, F // 256)
    def _(n):
        span = pl.ds(pl.multiple_of(n * 256, 256), 256)
        total = acc[:, span] + jnp.dot(
            tsel[:, :4 * TILE], fbuf[:4, :, span].reshape(4 * TILE, 256), preferred_element_type=F32
        )
        agg[0, :, span] = total.astype(BF)

    send_agg = remote(agg.at[0], agg.at[1], ags, agr, partner)
    send_agg.start()

    def half(h):
        for n in range(2):
            pieces = wall[h, 2 * n:2 * n + 2].reshape(256, F)
            pre = lax.dot_general(agg[0], pieces, (((1,), (1,)), ((), ())), preferred_element_type=F32)
            s = jax.nn.sigmoid(pre)
            outp[h, :, n * 256:(n + 1) * 256] = (pre * s).astype(BF)
            ct = cperm[h, :, n * 256:(n + 1) * 256].astype(F32)
            grad[h, :, n * 256:(n + 1) * 256] = (ct * s * (1.0 + pre * (1.0 - s))).astype(BF)

    half(other)
    send_g = remote(grad.at[other], gpart, gs, gr, partner)
    send_g.start()
    half(k)
    send_agg.wait_recv()
    send_g.wait_recv()

    def x1(d, block):
        return remote(s1x.at[block], r1x.at[d], a1s.at[d], a1r.at[d], device(xpeer(d), y, z, k))

    def y1(d, block):
        return remote(s1y.at[block], r1y.at[d], b1s.at[d], b1r.at[d], device(x, ypeer(d), z, k))

    for q in range(Y):
        lanes = slice(q * 128, (q + 1) * 128)
        term = lax.dot_general(
            grad[k, :, lanes], agg[0], (((0,), (0,)), ((), ())), preferred_element_type=F32
        ) + lax.dot_general(gpart[:, lanes], agg[1], (((0,), (0,)), ((), ())), preferred_element_type=F32)
        term = term.reshape(X, PIECE, F)
        dw[q] = term
        for p in range(X):
            s1x[p, q] = term[p, :, :H].astype(BF)
        s1y[q] = term[:, :, H:].astype(BF)

    for d in range(1, X):
        x1(d, xpeer(d)).start()
    for d in range(1, Y):
        y1(d, ypeer(d)).start()

    @pl.loop(0, F // 256)
    def _(n):
        span = pl.ds(pl.multiple_of(n * 256, 256), 256)
        outv[:, span] = (
            jnp.dot(outp[0], onehot[:H, span], preferred_element_type=F32)
            + jnp.dot(outp[1], onehot[H:, span], preferred_element_type=F32)
        ).astype(BF)

    save_out = pltpu.make_async_copy(outv, out, loc.at[4])
    save_out.start()

    for d in range(1, X):
        x1(d, xpeer(d)).wait_recv()
    for q in range(Y):
        total = dw[q, x][:, :H]
        for d in range(1, X):
            total = total + r1x[d, q].astype(F32)
        t2x[q] = total
        s2x[q] = total.astype(BF)

    def y2(d, block):
        return remote(s2x.at[block], r2x.at[d], a2s.at[d], a2r.at[d], device(x, ypeer(d), z, k))

    def x2(d, block):
        return remote(s2y.at[block], r2y.at[d], b2s.at[d], b2r.at[d], device(xpeer(d), y, z, k))

    for d in range(1, Y):
        y2(d, ypeer(d)).start()

    for d in range(1, Y):
        y1(d, ypeer(d)).wait_recv()
    for p in range(X):
        total = dw[y, p][:, H:]
        for d in range(1, Y):
            total = total + r1y[d, p].astype(F32)
        t2y[p] = total
        s2y[p] = total.astype(BF)
    for d in range(1, X):
        x2(d, xpeer(d)).start()

    for d in range(1, Y):
        y2(d, ypeer(d)).wait_recv()
    left = t2x[y]
    for d in range(1, Y):
        left = left + r2x[d].astype(F32)
    zs[:, :, :H] = left.reshape(Z, 2, H)
    for d in range(1, X):
        x2(d, xpeer(d)).wait_recv()
    right = t2y[x]
    for d in range(1, X):
        right = right + r2y[d].astype(F32)
    zs[:, :, H:] = right.reshape(Z, 2, H)

    def z3(d):
        return remote(zs.at[zpeer(d)], zr.at[d], z3s.at[d], z3r.at[d], device(x, y, zpeer(d), k))

    @pl.loop(1, Z)
    def _(d):
        z3(d).start()

    total = zs[z]
    for d in range(1, Z):
        z3(d).wait_recv()
        total = total + zr[d]
    wgrad[...] = total

    @pl.loop(1, Z)
    def _(d):
        wz_copy(d, z).wait_send()
        z3(d).wait_send()

    @pl.loop(0, CHUNKS)
    def _(j):
        f2(j).wait_send()
        f4(j, same).wait_send()
        f5(j, same, cross).wait_send()
        f6(j, cross).wait_send()

    f1.wait_send()
    f3.wait_send()
    wp.wait_send()
    send_agg.wait_send()
    send_g.wait_send()
    for d in range(1, X):
        wx(d, x).wait_send()
        x1(d, xpeer(d)).wait_send()
        x2(d, xpeer(d)).wait_send()
    for d in range(1, Y):
        wy(d, y).wait_send()
        y1(d, ypeer(d)).wait_send()
        y2(d, ypeer(d)).wait_send()
    save_out.wait()


def local(features, tiles, tile_cols, tile_count, weight, cotangent):
    anywhere = pl.BlockSpec(memory_space=pl.ANY)
    scalars = pl.BlockSpec(memory_space=pltpu.SMEM)
    dma = pltpu.SemaphoreType.DMA
    vmem = pltpu.VMEM
    return tuple(pl.pallas_call(
        kernel,
        out_shape=(
            jax.ShapeDtypeStruct((TILE, F), BF),
            jax.ShapeDtypeStruct((2, F), F32),
        ),
        in_specs=[anywhere, anywhere, scalars, scalars, anywhere, anywhere],
        out_specs=(anywhere, pl.BlockSpec(memory_space=pltpu.VMEM)),
        scratch_shapes=[
            vmem((SLOTS, TILE, F), BF),
            vmem((SLOTS, TILE, TILE), BF),
            vmem((TILE, SLOTS * TILE), BF),
            vmem((TILE, F), BF),
            vmem((C, TILE, H), BF),
            vmem((F, F), BF),
            vmem((Z, 2, F), BF),
            vmem((C, Y, X, PIECE, F), BF),
            vmem((TILE, F), F32),
            vmem((C, TILE, F), BF),
            vmem((C, TILE, H), BF),
            vmem((TILE, H), BF),
            vmem((C, TILE, H), BF),
            vmem((TILE, F), BF),
            vmem((Y, X, PIECE, F), F32),
            vmem((X, Y, PIECE, H), BF),
            vmem((X, Y, PIECE, H), BF),
            vmem((Y, X, PIECE, H), BF),
            vmem((Y, X, PIECE, H), BF),
            vmem((Y, PIECE, H), F32),
            vmem((X, PIECE, H), F32),
            vmem((Y, PIECE, H), BF),
            vmem((Y, PIECE, H), BF),
            vmem((X, PIECE, H), BF),
            vmem((X, PIECE, H), BF),
            vmem((Z, 2, F), F32),
            vmem((Z, 2, F), F32),
            dma((5,)),
            dma, dma,
            dma((CHUNKS,)), dma((CHUNKS,)),
            dma, dma,
            dma((CHUNKS,)), dma((CHUNKS,)),
            dma((CHUNKS,)), dma((CHUNKS,)),
            dma((CHUNKS,)), dma((CHUNKS,)),
            dma((Z,)), dma((Z,)),
            dma((Y,)), dma((Y,)),
            dma((X,)), dma((X,)),
            dma, dma,
            dma, dma,
            dma, dma,
            dma((X,)), dma((X,)),
            dma((Y,)), dma((Y,)),
            dma((Y,)), dma((Y,)),
            dma((X,)), dma((X,)),
            dma((Z,)), dma((Z,)),
        ],
        compiler_params=pltpu.CompilerParams(
            collective_id=0, has_side_effects=True, vmem_limit_bytes=56 << 20
        ),
    )(features, tiles, tile_cols, tile_count, weight, cotangent))


def solution(mesh):
    in_specs = (
        P(("rows", "blk"), None),
        P(("rows", "blk"), None, None, None),
        P(("rows", "blk"), None),
        P(("rows", "blk")),
        P(("rows", "blk"), None),
        P(("rows", "blk"), None),
    )
    out_specs = (P(("rows", "blk"), None), P(("rows", "blk"), None))
    return jax.shard_map(local, mesh=mesh, in_specs=in_specs, out_specs=out_specs, check_vma=False)
```

time: 1390 us -> 123 us (0.09)
  the two profiles are of different devices: /device:TPU:2 before, /device:TPU:4 now
where the time goes in v1:
time: 123 us
  Pallas kernels  119 us (97%)
  local copies, waits for them, and re-layouts  2.48 us (2%)
  between operations  1.29 us (1%)
    pallas_call x1, Pallas kernels, local(): pl.pallas_call(kernel, out_shape=(jax.ShapeDtypeStruct((TILE, F), BF), ja...  119 us
    unnamed x4, local copies, waits for them, and re-layouts  2.48 us

profile of v1, /device:TPU:4, one launch (start us, length us, event | category | flops | bytes accessed | tf_op | source)
XLA Modules:
  0.0 122.8 jit_solution(1960492609026550491)
XLA Ops:
  1.3 119.1 %shard_map.77 = (bf16[256,1024]{1,0:T(8,128)(2,1)}, f32[2,1024]{1,0:T(2,128)}) custom-call(bf16[256,1024]{1,0:T(8,128)(2,1)} %feat.1, bf16[1,7,256,256]{3,2,1,0:T(8,128)(2,1)} %tiles.1, s32[1,7]{1,0:T(1,128)} %cols.1, s32[1]{0:T(128)S(6)} %copy.10.count, bf16[2,1024]{1,0:T(2,128)(2,1)} %weight.1, bf16[256,1024]{1,0:T(8,128)(2,1)} %cot.1), custom_call_target="tpu_custom_call" | custom-call | tf_op jit(solution)/shard_map/pallas_call | solution.py:390
  120.3 0.0 copy-start
  120.3 1.9 %copy.11 = bf16[256,1024]{1,0:T(8,128)(2,1)} copy(bf16[256,1024]{1,0:T(8,128)(2,1)} %get-tuple-element.4) | data formatting | bytes 1048576
  122.2 0.0 copy-done
  122.2 0.6 copy.12
Async XLA Ops:
  120.3 1.9 %copy-start = (f32[2,1024]{1,0:T(2,128)S(1)}, f32[2,1024]{1,0:T(2,128)}, u32[]{:S(2)}) copy-start(f32[2,1024]{1,0:T(2,128)} %get-tuple-element.5) | copy-start | bytes 24580

commit v2 on v1

--- a/solution.py
+++ b/solution.py
@@ -15,6 +15,7 @@
 F = 1024
 SLOTS = 7
 CHUNKS = 8
+DEPTH = 2
 CROWS = TILE // CHUNKS
 H = F // 2
 PIECE = 2 * Z
@@ -104,7 +105,7 @@
         rows = pl.ds(j * CROWS, CROWS)
         return remote(feat.at[rows], fbuf.at[same_there, rows], f2s.at[j], f2r.at[j], far)
 
-    @pl.loop(0, CHUNKS)
+    @pl.loop(0, DEPTH)
     def _(j):
         f2(j).start()
 
@@ -156,13 +157,13 @@
 
     wall[k, y, x] = wz[...].astype(F32).reshape(PIECE, F).astype(BF)
 
-    def wy(d, dst):
+    def wx(d, dst):
         return remote(
-            wall.at[k, dst, x], wall.at[k, dst, x], wys.at[d], wyr.at[d], device(x, ypeer(d), z, k)
-        )
-
-    for d in range(1, Y):
-        wy(d, y).start()
+            wall.at[k, y, dst], wall.at[k, y, dst], wxs.at[d], wxr.at[d], device(xpeer(d), y, z, k)
+        )
+
+    for d in range(1, X):
+        wx(d, x).start()
 
     load_c.wait()
     for h in range(C):
@@ -170,16 +171,16 @@
             cbuf[...], onehot[h * H:(h + 1) * H, :], (((1,), (1,)), ((), ())), preferred_element_type=F32
         ).astype(BF)
 
-    for d in range(1, Y):
-        wy(d, ypeer(Y - d)).wait_recv()
-
-    def wx(d, dst):
+    for d in range(1, X):
+        wx(d, xpeer(X - d)).wait_recv()
+
+    def wy(d, dst):
         return remote(
-            wall.at[k, :, dst], wall.at[k, :, dst], wxs.at[d], wxr.at[d], device(xpeer(d), y, z, k)
-        )
-
-    for d in range(1, X):
-        wx(d, x).start()
+            wall.at[k, dst], wall.at[k, dst], wys.at[d], wyr.at[d], device(x, ypeer(d), z, k)
+        )
+
+    for d in range(1, Y):
+        wy(d, y).start()
 
     load_f.wait()
     remote(feat, fbuf.at[4 + other], f1s, f1r, partner).wait_recv()
@@ -210,6 +211,11 @@
         f4(j, same).start()
         f5(j, same, cross).start()
 
+        @pl.when(j + DEPTH < CHUNKS)
+        def _():
+            f2(j).wait_send()
+            f2(j + DEPTH).start()
+
     def cross_arrival(j):
         f5(j, same, cross).wait_recv()
         f6(j, cross).start()
@@ -221,8 +227,8 @@
         far_arrival(j)
         cross_arrival(j - 1)
 
-    for d in range(1, X):
-        wx(d, xpeer(X - d)).wait_recv()
+    for d in range(1, Y):
+        wy(d, ypeer(Y - d)).wait_recv()
     wp = remote(wall.at[k], wall.at[k], wps, wpr, partner)
     wp.start()
 
@@ -361,11 +367,12 @@
 
     @pl.loop(0, CHUNKS)
     def _(j):
-        f2(j).wait_send()
         f4(j, same).wait_send()
         f5(j, same, cross).wait_send()
         f6(j, cross).wait_send()
 
+    for j in range(CHUNKS - DEPTH, CHUNKS):
+        f2(j).wait_send()
     f1.wait_send()
     f3.wait_send()
     wp.wait_send()

time: 123 us -> 116 us (0.943)
  the two profiles are of different devices: /device:TPU:4 before, /device:TPU:32 now
where the time goes in v2:
time: 116 us; the launch traced here: 115 us
  Pallas kernels  112 us (97%)
  local copies, waits for them, and re-layouts  2.48 us (2%)
  between operations  1.29 us (1%)
    pallas_call x1, Pallas kernels, local(): pl.pallas_call(kernel, out_shape=(jax.ShapeDtypeStruct((TILE, F), BF), ja...  112 us
    unnamed x4, local copies, waits for them, and re-layouts  2.48 us

profile of v2, /device:TPU:32, one launch (start us, length us, event | category | flops | bytes accessed | tf_op | source)
XLA Modules:
  0.0 115.4 jit_solution(16738803673218014710)
XLA Ops:
  1.3 111.6 %shard_map.77 = (bf16[256,1024]{1,0:T(8,128)(2,1)}, f32[2,1024]{1,0:T(2,128)}) custom-call(bf16[256,1024]{1,0:T(8,128)(2,1)} %feat.1, bf16[1,7,256,256]{3,2,1,0:T(8,128)(2,1)} %tiles.1, s32[1,7]{1,0:T(1,128)} %cols.1, s32[1]{0:T(128)S(6)} %copy.10.count, bf16[2,1024]{1,0:T(2,128)(2,1)} %weight.1, bf16[256,1024]{1,0:T(8,128)(2,1)} %cot.1), custom_call_target="tpu_custom_call" | custom-call | tf_op jit(solution)/shard_map/pallas_call | solution.py:397
  112.9 0.0 copy-start
  112.9 1.9 %copy.11 = bf16[256,1024]{1,0:T(8,128)(2,1)} copy(bf16[256,1024]{1,0:T(8,128)(2,1)} %get-tuple-element.4) | data formatting | bytes 1048576
  114.8 0.0 copy-done
  114.8 0.6 copy.12
Async XLA Ops:
  112.9 1.9 %copy-start = (f32[2,1024]{1,0:T(2,128)S(1)}, f32[2,1024]{1,0:T(2,128)}, u32[]{:S(2)}) copy-start(f32[2,1024]{1,0:T(2,128)} %get-tuple-element.5) | copy-start | bytes 24580
